TPU v7x, 32 devices: a whole 2x2x4 slice. The times are simulated.
32 devices in a mesh: row: 4 (over x, core), col: 8 (over z, y).
Axes of the slice: x: 2, y: 2, z: 4, core: 2. Of those that a mesh axis runs over, the one named last changes fastest.
Arguments:
- object_field: float32 [2, 2048, 4096], P(None, 'row', 'col'), may hold values from -6 to 6
- probe: float32 [2, 256, 256], replicated, may hold values from -6 to 6
- dual: float32 [2, 4, 8, 4, 256, 256], P(None, 'row', 'col'), may hold values from -4 to 4
- amplitude: float32 [4, 8, 4, 256, 256], P('row', 'col'), may hold values from 0.1 to 3
- offsets: int32 [2, 4, 8, 4], P(None, 'row', 'col'), may hold values from 0 to 511
- live: int32 [4, 8], P('row', 'col'), may hold values from 1 to 4, as said below
Outputs:
- object_new: float32 [2, 2048, 4096], P(None, 'row', 'col')
- dual_new: float32 [2, 4, 8, 4, 256, 256], P(None, 'row', 'col')
Inputs may be any that keep to these rules, and one draw needn't show every extreme that they name: `offsets`: each slot's probe centre lies inside its own tile. `live`: the used slots of a tile are its first ones; some tile uses all 4 slots.
All inputs are finite; a program needn't handle non-finite values.
Results may differ from a plain program's by a relative error of at most 0.00022.
Values sent between devices are 32-bit elements; how exact they have to be, the bound alone decides.
A program may use at most 128 MiB of HBM per device.

v0:
```python
import functools
import math

import jax
import jax.numpy as jnp
import numpy as np
from jax import lax
from jax.experimental import pallas as pl
from jax.experimental.pallas import tpu as pltpu
from jax.sharding import PartitionSpec as P

FLOOR = 0.1
BETA = 1.0
LANES = 128
ROWS = 8
MIB = 1 << 20
F32 = jnp.float32
BF16 = jnp.bfloat16
ANY = pl.BlockSpec(memory_space=pl.ANY)
VM = pl.BlockSpec(memory_space=pltpu.VMEM)
SM = pl.BlockSpec(memory_space=pltpu.SMEM)


def tables(size):
    n = size // 2
    k = np.arange(n)
    angle = 2.0 * math.pi * ((k[:, None] * k[None, :]) % n) / n
    c, s = np.cos(angle) / math.sqrt(size), np.sin(angle) / math.sqrt(size)
    fwd = np.block([[c, s], [-s, c]])
    inv = np.block([[c, -s], [s, c]])
    parts = []
    for full in (fwd, inv):
        hi = full.astype(np.float32).astype(BF16)
        parts += [hi, (full - hi.astype(np.float64)).astype(np.float32).astype(BF16)]
    perm = np.zeros((size, size), np.float32)
    perm[2 * k, k] = 1.0
    perm[2 * k + 1, n + k] = 1.0
    tw = 2.0 * math.pi * k / size
    ct, st = np.cos(tw).astype(np.float32), np.sin(tw).astype(np.float32)
    rows = np.stack([np.broadcast_to(ct[:, None], (n, size)), np.broadcast_to(st[:, None], (n, size))])
    cols = np.stack([np.broadcast_to(ct[None, :], (size, n)), np.broadcast_to(st[None, :], (size, n))])
    return [jnp.asarray(np.stack(parts)), jnp.asarray(perm.astype(BF16)), jnp.asarray(rows), jnp.asarray(cols)]


def split(x):
    hi = x.astype(BF16)
    return hi, (x - hi.astype(F32)).astype(BF16)


def dot(a, b):
    return jnp.dot(a, b, preferred_element_type=F32)


def left_dot(wh, wl, x):
    xh, xl = split(x)
    return dot(wl, xh) + dot(wh, xl) + dot(wh, xh)


def right_dot(x, wh, wl):
    xh, xl = split(x)
    return dot(xh, wl) + dot(xl, wh) + dot(xh, wh)


def cat(parts, axis):
    return jnp.concatenate(parts, axis=axis)


def load_window(ext, channel, top, left, size):
    row = pl.multiple_of((top // ROWS) * ROWS, ROWS)
    base = pl.multiple_of((left // LANES) * LANES, LANES)
    width, height = size + LANES, size + ROWS
    wide = ext[channel, pl.ds(row, height), pl.ds(base, width)]
    wide = pltpu.roll(wide, (width - (left - base)) % width, 1)[:, :size]
    return pltpu.roll(wide, (height - (top - row)) % height, 0)[:size]


def add_window(acc, channel, top, left, value):
    size = value.shape[0]
    row = pl.multiple_of((top // ROWS) * ROWS, ROWS)
    base = pl.multiple_of((left // LANES) * LANES, LANES)
    width, height = size + LANES, size + ROWS
    wide = cat([value, jnp.zeros((ROWS, size), F32)], 0)
    wide = pltpu.roll(wide, top - row, 0)
    wide = cat([wide, jnp.zeros((height, LANES), F32)], 1)
    wide = pltpu.roll(wide, left - base, 1)
    acc[channel, pl.ds(row, height), pl.ds(base, width)] += wide


def clear_beyond(grid, tile, half, frame):
    end = half + tile
    strips = (
        ("up", slice(0, half), slice(None)),
        ("down", slice(end, None), slice(None)),
        ("left", slice(half, end), slice(0, half)),
        ("right", slice(half, end), slice(end, None)),
    )
    for side, rows, cols in strips:

        @pl.when(jnp.logical_not(grid.has[side]))
        def _():
            frame[:, rows, cols] = jnp.zeros_like(frame[:, rows, cols])

    for up, rows in (("up", slice(0, half)), ("down", slice(end, None))):
        for side, cols in (("left", slice(0, half)), ("right", slice(end, None))):

            @pl.when(grid.has[up] & jnp.logical_not(grid.has[side]))
            def _():
                frame[:, rows, cols] = jnp.zeros_like(frame[:, rows, cols])


class Grid:
    def __init__(self, send, recv):
        row, col = lax.axis_index("row"), lax.axis_index("col")
        self.has = {
            "up": row > 0,
            "down": row < lax.axis_size("row") - 1,
            "left": col > 0,
            "right": col < lax.axis_size("col") - 1,
        }
        self.peer = {"up": {"row": row - 1}, "down": {"row": row + 1}, "left": {"col": col - 1}, "right": {"col": col + 1}}
        self.back = {"up": "down", "down": "up", "left": "right", "right": "left"}
        self.send, self.recv = send, recv
        self.count = 0

    def greet(self):
        barrier = pltpu.get_barrier_semaphore()
        for side in self.has:

            @pl.when(self.has[side])
            def _():
                pl.semaphore_signal(barrier, inc=1, device_id=self.peer[side], device_id_type=pl.DeviceIdType.MESH)

        pl.semaphore_wait(barrier, sum(h.astype(jnp.int32) for h in self.has.values()))

    def message(self, side, src, dst, also=None):
        at = self.count
        self.count += 1
        copy = pltpu.make_async_remote_copy(
            src_ref=src,
            dst_ref=dst,
            send_sem=self.send.at[at],
            recv_sem=self.recv.at[at],
            device_id=self.peer[side],
            device_id_type=pl.DeviceIdType.MESH,
        )
        goes, comes = self.has[side], self.has[self.back[side]]
        if also is not None:
            goes, comes = goes & self.has[also], comes & self.has[also]
        return copy, goes, comes


def when(cond, act):
    if cond is True:
        act()
    else:
        pl.when(cond)(act)


def start(*messages):
    for copy, goes, _ in messages:
        pl.when(goes)(copy.start)


def arrive(*messages):
    for copy, _, comes in messages:
        pl.when(comes)(copy.wait_recv)


def leave(*messages):
    for copy, goes, _ in messages:
        pl.when(goes)(copy.wait_send)


def column_messages(grid, tile, half, src, frame):
    size, end = 2 * half, half + tile
    tops, bottoms, mids = slice(0, half), slice(tile - half, tile), slice(half, tile - half)
    ends, inner = [], []
    for rows, store, group in (
        (tops, slice(half, size), ends),
        (bottoms, slice(tile, end), ends),
        (mids, slice(size, tile), inner),
    ):
        group.append(grid.message("left", src.at[:, rows, :half], frame.at[:, store, end:]))
        group.append(grid.message("right", src.at[:, rows, tile - half :], frame.at[:, store, :half]))
    return ends, inner


def row_messages(grid, tile, half, src, frame):
    end = half + tile
    return [
        grid.message("up", src.at[:, :half, :], frame.at[:, end:, half:end]),
        grid.message("down", src.at[:, tile - half :, :], frame.at[:, :half, half:end]),
    ]


def corner_messages(grid, tile, half, frame):
    size, end = 2 * half, half + tile
    out = []
    for side, cols in (("left", slice(0, half)), ("right", slice(end, None))):
        out.append(grid.message("up", frame.at[:, half:size, cols], frame.at[:, end:, cols], also=side))
        out.append(grid.message("down", frame.at[:, tile:end, cols], frame.at[:, :half, cols], also=side))
    return out


def halo_kernel(tile, half, cells, info, frame, infos, send, recv, local):
    grid = Grid(send, recv)
    ends, inner = column_messages(grid, tile, half, cells, frame)
    rows = row_messages(grid, tile, half, cells, frame)
    corners = corner_messages(grid, tile, half, frame)
    tags = [
        grid.message("left", info.at[0], infos.at[1, 2]),
        grid.message("right", info.at[0], infos.at[1, 0]),
    ]
    bands = [
        grid.message("up", infos.at[1], infos.at[2]),
        grid.message("down", infos.at[1], infos.at[0]),
    ]
    fills = [
        (pltpu.make_async_copy(info.at[0], infos.at[1, 1], local.at[0]), True),
        (pltpu.make_async_copy(info.at[1], infos.at[1, 0], local.at[1]), jnp.logical_not(grid.has["left"])),
        (pltpu.make_async_copy(info.at[1], infos.at[1, 2], local.at[2]), jnp.logical_not(grid.has["right"])),
        (pltpu.make_async_copy(info.at[pl.ds(1, 3)], infos.at[0], local.at[3]), jnp.logical_not(grid.has["up"])),
        (pltpu.make_async_copy(info.at[pl.ds(1, 3)], infos.at[2], local.at[4]), jnp.logical_not(grid.has["down"])),
        (pltpu.make_async_copy(cells, frame.at[:, half : half + tile, half : half + tile], local.at[5]), True),
    ]
    for copy, cond in fills:
        when(cond, copy.start)
    grid.greet()
    start(*tags, *ends, *inner, *rows)
    clear_beyond(grid, tile, half, frame)
    for copy, cond in fills:
        when(cond, copy.wait)
    arrive(*tags)
    start(*bands)
    arrive(*ends)
    start(*corners)
    arrive(*inner, *rows, *bands, *corners)
    leave(*tags, *ends, *inner, *rows, *bands, *corners)


def update_kernel(tile, half, *refs):
    acc, cells, weight, frame = refs[:4]
    fa, fb, g_lm, g_rm, g_le, g_re, s_le, s_re, send, recv = refs[4:]
    size, end = 2 * half, half + tile
    grid = Grid(send, recv)
    has = grid.has
    val = frame.at[:, half:end, half:end]
    up = grid.message("up", acc.at[:, :half, :], fb)
    down = grid.message("down", acc.at[:, end:, :], fa)
    mids = [
        grid.message("left", acc.at[:, size:tile, :half], g_rm),
        grid.message("right", acc.at[:, size:tile, end:], g_lm),
    ]
    ends = [grid.message("left", s_le, g_re), grid.message("right", s_re, g_le)]
    new_ends, new_inner = column_messages(grid, tile, half, val, frame)
    new_rows = row_messages(grid, tile, half, val, frame)
    corners = corner_messages(grid, tile, half, frame)
    grid.greet()
    start(up, down, *mids)
    clear_beyond(grid, tile, half, frame)
    for side, buffers in (("up", (fa,)), ("down", (fb,)), ("left", (g_lm, g_le)), ("right", (g_rm, g_re))):

        @pl.when(jnp.logical_not(has[side]))
        def _():
            for b in buffers:
                b[...] = jnp.zeros_like(b)

    arrive(up, down)
    for ch in range(2):
        s_le[ch, 0] = acc[ch, half:size, :half] + fa[ch, :, :half]
        s_le[ch, 1] = acc[ch, tile:end, :half] + fb[ch, :, :half]
        s_re[ch, 0] = acc[ch, half:size, end:] + fa[ch, :, end:]
        s_re[ch, 1] = acc[ch, tile:end, end:] + fb[ch, :, end:]
    start(*ends)
    tops, bottoms, inner = slice(0, half), slice(tile - half, tile), slice(half, tile - half)
    heads, tails = slice(0, half), slice(tile - half, tile)

    def moved(at):
        return slice(at.start + half, at.stop + half)

    def settle(ch, rows, cols, more):
        total = acc[ch, moved(rows), moved(cols)] + BETA * cells[ch, rows, cols]
        for m in more:
            total = total + m
        frame[ch, moved(rows), moved(cols)] = total / weight[rows, cols]

    for ch in range(2):
        settle(ch, inner, inner, ())
        settle(ch, tops, inner, (fa[ch, :, size:tile],))
        settle(ch, bottoms, inner, (fb[ch, :, size:tile],))
    arrive(*mids)
    for ch in range(2):
        settle(ch, inner, heads, (g_lm[ch],))
        settle(ch, inner, tails, (g_rm[ch],))
    start(*new_inner)
    arrive(*ends)
    for ch in range(2):
        settle(ch, tops, heads, (fa[ch, :, half:size], g_le[ch, 0]))
        settle(ch, bottoms, heads, (fb[ch, :, half:size], g_le[ch, 1]))
        settle(ch, tops, tails, (fa[ch, :, tile:end], g_re[ch, 0]))
        settle(ch, bottoms, tails, (fb[ch, :, tile:end], g_re[ch, 1]))
    start(*new_ends, *new_rows)
    arrive(*new_ends)
    start(*corners)
    arrive(*new_inner, *new_rows, *corners)
    leave(up, down, *mids, *ends, *new_ends, *new_inner, *new_rows, *corners)


def add_weights(tile, half, slots, info, acc, power):
    size = 2 * half

    def body(index, carry):
        owner = index // slots
        slot = index % slots
        r, c = owner // 3, owner % 3
        top = info[r, c, 0, slot] + (r - 1) * tile + half
        left = info[r, c, 0, slots + slot] + (c - 1) * tile + half
        live = info[r, c, 0, 2 * slots]
        hit = (slot < live) & (top > 0) & (top < size + tile) & (left > 0) & (left < size + tile)

        @pl.when(hit)
        def _():
            add_window(acc, 0, top, left, power[...])

        return carry

    lax.fori_loop(0, 9 * slots, body, 0)


def project_kernel(tile, half, info, *refs):
    ext, probe, dual, amp, wt, perm, twr, twc = refs[:8]
    base, acc, weight, heavy, power, strips = refs[8:]
    slots = dual.shape[1]
    size = 2 * half
    acc[...] = jnp.zeros_like(acc)
    heavy[...] = jnp.full_like(heavy, BETA)
    power[...] = probe[0] * probe[0] + probe[1] * probe[1]
    add_weights(tile, half, slots, info, heavy, power)
    weight[...] = heavy[0, size : size + tile, size : size + tile]
    live = info[1, 1, 0, 2 * slots]

    def skip(slot, carry):
        base[:, slot] = dual[:, slot]
        return carry

    def step(slot, carry):
        top = info[1, 1, 0, slot]
        left = info[1, 1, 0, slots + slot]
        pr, pi = probe[0], probe[1]
        sr = load_window(ext, 0, top, left, size)
        si = load_window(ext, 1, top, left, size)
        re = pr * sr - pi * si + dual[0, slot]
        im = pr * si + pi * sr + dual[1, slot]
        fh, fl, ih, il = wt[0], wt[1], wt[2], wt[3]
        cr, sr_ = twr[0], twr[1]
        cc, sc = twc[0], twc[1]
        dr, di = re[:half] - re[half:], im[:half] - im[half:]
        x = cat(
            [
                cat([re[:half] + re[half:], dr * cr + di * sr_], 1),
                cat([im[:half] + im[half:], di * cr - dr * sr_], 1),
            ],
            0,
        )
        y = left_dot(fh, fl, x)
        re = cat([y[:half, :size], y[:half, size:]], 0)
        im = cat([y[half:, :size], y[half:, size:]], 0)
        dr, di = re[:, :half] - re[:, half:], im[:, :half] - im[:, half:]
        x = cat(
            [
                cat([re[:, :half] + re[:, half:], im[:, :half] + im[:, half:]], 1),
                cat([dr * cc + di * sc, di * cc - dr * sc], 1),
            ],
            0,
        )
        s = right_dot(x, ih, il)
        for c in range(size // LANES):
            strips[c] = amp[slot, :, c * LANES : (c + 1) * LANES]
        a = cat(
            [
                cat([strips[c, pl.ds(first, half, stride=2), :] for c in range(size // LANES)], 1)
                for first in range(2)
            ],
            0,
        )
        ah, al = split(a)
        a = dot(ah, perm[...]) + dot(al, perm[...])
        a = cat([a[:, :half], a[:, half:]], 0)
        sre, sim = s[:, :half], s[:, half:]
        fac = a * lax.rsqrt(jnp.maximum(sre * sre + sim * sim, FLOOR * FLOOR))
        x = cat([sre * fac, sim * fac], 1)
        z = right_dot(x, fh, fl)
        er, ei = z[:size, :half], z[:size, half:]
        orr, oi = z[size:, :half], z[size:, half:]
        tr, ti = orr * cc - oi * sc, oi * cc + orr * sc
        re = cat([er + tr, er - tr], 1)
        im = cat([ei + ti, ei - ti], 1)
        x = cat([cat([re[:half], re[half:]], 1), cat([im[:half], im[half:]], 1)], 0)
        y = left_dot(ih, il, x)
        er, ei = y[:half, :size], y[half:, :size]
        orr, oi = y[:half, size:], y[half:, size:]
        tr, ti = orr * cr - oi * sr_, oi * cr + orr * sr_
        dr = cat([er + tr, er - tr], 0) - dual[0, slot]
        di = cat([ei + ti, ei - ti], 0) - dual[1, slot]
        base[0, slot] = -dr
        base[1, slot] = -di
        add_window(acc, 0, top, left, pr * dr + pi * di)
        add_window(acc, 1, top, left, pr * di - pi * dr)
        return carry

    lax.fori_loop(live, slots, skip, 0)
    lax.fori_loop(0, live, step, 0)


def dual_kernel(tile, half, info, ext, probe, base, out, new, ready, sems):
    slots = base.shape[1]
    size = 2 * half
    keep = pltpu.make_async_copy(ext.at[:, half : half + tile, half : half + tile], new, sems.at[slots])
    keep.start()
    copies = []
    for slot in range(slots):
        copy = pltpu.make_async_copy(ready.at[slot], out.at[:, slot], sems.at[slot])
        copies.append(copy)
        active = slot < info[1, 1, 0, 2 * slots]

        @pl.when(jnp.logical_not(active))
        def _():
            ready[slot] = base[:, slot]

        @pl.when(active)
        def _():
            top = info[1, 1, 0, slot]
            left = info[1, 1, 0, slots + slot]
            pr, pi = probe[0], probe[1]
            sr = load_window(ext, 0, top, left, size)
            si = load_window(ext, 1, top, left, size)
            ready[slot, 0] = base[0, slot] + (pr * sr - pi * si)
            ready[slot, 1] = base[1, slot] + (pr * si + pi * sr)

        copy.start()
    for copy in copies:
        copy.wait()
    keep.wait()


def shards(object_field, probe, dual, amplitude, offsets, live):
    tile = object_field.shape[1]
    size = probe.shape[1]
    half = size // 2
    slots = dual.shape[3]
    wide = tile + size
    mid = tile - size
    lam = dual.reshape(2, slots, size, size)
    amps = amplitude.reshape(slots, size, size)
    sd = lambda *shape: jax.ShapeDtypeStruct(shape, F32)
    dma = lambda n: pltpu.SemaphoreType.DMA((n,))

    own = jnp.concatenate([offsets[0, 0, 0], offsets[1, 0, 0], live[0]])
    tag = jnp.pad(own[None, None], ((0, 3), (0, ROWS - 1), (0, LANES - own.shape[0])))

    frame, infos = pl.pallas_call(
        functools.partial(halo_kernel, tile, half),
        out_shape=(sd(2, wide, wide), jax.ShapeDtypeStruct((3, 3, ROWS, LANES), jnp.int32)),
        in_specs=[ANY, ANY],
        out_specs=(VM, ANY),
        scratch_shapes=[dma(16), dma(16), dma(6)],
        compiler_params=pltpu.CompilerParams(collective_id=0, has_side_effects=True, vmem_limit_bytes=2 * MIB),
        cost_estimate=pl.CostEstimate(flops=0, bytes_accessed=80_000_000, transcendentals=0),
        name="halo",
    )(object_field, tag)

    cost = lambda size: pl.CostEstimate(flops=0, bytes_accessed=size, transcendentals=0)
    base, acc, weight = pl.pallas_call(
        functools.partial(project_kernel, tile, half),
        out_shape=(sd(2, slots, size, size), sd(2, wide, wide), sd(tile, tile)),
        in_specs=[SM] + [VM] * 8,
        out_specs=(VM, VM, VM),
        scratch_shapes=[
            pltpu.VMEM((1, tile + 2 * size, tile + 2 * size), F32),
            pltpu.VMEM((size, size), F32),
            pltpu.VMEM((size // LANES, size, LANES), F32),
        ],
        compiler_params=pltpu.CompilerParams(vmem_limit_bytes=16 * MIB),
        cost_estimate=cost(30_000_000),
        name="project",
    )(infos, frame, probe, lam, amps, *tables(size))

    strip, side, end = (2, half, wide), (2, mid, half), (2, 2, half, half)
    frame = pl.pallas_call(
        functools.partial(update_kernel, tile, half),
        out_shape=sd(2, wide, wide),
        in_specs=[VM] * 3,
        out_specs=VM,
        scratch_shapes=[pltpu.VMEM(x, F32) for x in (strip, strip, side, side, end, end, end, end)] + [dma(18), dma(18)],
        compiler_params=pltpu.CompilerParams(collective_id=1, has_side_effects=True, vmem_limit_bytes=8 * MIB),
        cost_estimate=cost(150_000_000),
        name="update",
    )(acc, object_field, weight)

    dual_new, new = pl.pallas_call(
        functools.partial(dual_kernel, tile, half),
        out_shape=(sd(2, slots, size, size), sd(2, tile, tile)),
        in_specs=[SM, VM, VM, VM],
        out_specs=(ANY, ANY),
        scratch_shapes=[pltpu.VMEM((slots, 2, size, size), F32), dma(slots + 1)],
        compiler_params=pltpu.CompilerParams(vmem_limit_bytes=12 * MIB),
        name="renew",
    )(infos, frame, probe, base)
    return new, dual_new.reshape(dual.shape)


def solution(mesh):
    placed = (
        P(None, "row", "col"),
        P(),
        P(None, "row", "col", None, None, None),
        P("row", "col", None, None, None),
        P(None, "row", "col", None),
        P("row", "col"),
    )
    return jax.shard_map(
        shards,
        mesh=mesh,
        in_specs=placed,
        out_specs=(P(None, "row", "col"), P(None, "row", "col", None, None, None)),
        check_vma=False,
    )
```

profile of v0, /device:TPU:13, one launch (start us, length us, event | category | flops | bytes accessed | tf_op | source)
XLA Modules:
  0.0 109.5 jit_solution(2887371321579839522)
XLA Ops:
  1.3 0.7 slice_bitcast_fusion.1
  2.0 0.1 add_bitcast_fusion
  2.0 0.0 copy-start
  2.0 1.6 %copy-done = f32[2,512,512]{2,1,0:T(8,128)S(1)} copy-done((f32[2,512,512]{2,1,0:T(8,128)S(1)}, f32[2,512,512]{2,1,0:T(8,128)}, u32[]{:S(2)}) %copy-start) | copy-done | bytes 2097176
  3.6 0.0 copy-start.2
  3.6 0.0 copy-start.4
  3.6 0.0 copy-start.5
  3.6 27.1 %halo.1 = (f32[2,768,768]{2,1,0:T(8,128)S(1)}, s32[3,3,8,128]{3,2,1,0:T(8,128)S(1)}) custom-call(f32[2,512,512]{2,1,0:T(8,128)S(1)} %copy-done, s32[4,8,128]{2,1,0:T(8,128)S(1)} %pad.4.info), custom_call_target="tpu_custom_call" | custom-call | bytes 80000000 | tf_op jit(solution)/shard_map/halo/pallas_call | solution.py:461
  30.7 0.0 copy-done.2
  30.7 0.0 copy-done.4
  30.7 0.0 copy-done.5
  30.7 0.0 copy-start.3
  30.8 1.6 %copy-done.3 = f32[2,1,1,4,256,256]{5,4,3,2,1,0:T(8,128)S(1)} copy-done((f32[2,1,1,4,256,256]{5,4,3,2,1,0:T(8,128)S(1)}, f32[2,1,1,4,256,256]{5,4,3,2,1,0:T(8,128)}, u32[]{:S(2)}) %copy-start.3) | copy-done | bytes 2097176
  32.3 0.0 copy-start.6
  32.3 0.9 copy-done.6
  33.3 0.0 copy-start.7
  33.3 0.9 copy-done.7
  34.2 0.0 copy-start.8
  34.2 0.9 copy-done.8
  35.1 0.0 copy-start.1
  35.2 15.9 %project.1 = (f32[2,4,256,256]{3,2,1,0:T(8,128)S(1)}, f32[2,768,768]{2,1,0:T(8,128)S(1)}, f32[512,512]{1,0:T(8,128)S(1)}) custom-call(s32[3,3,8,128]{3,2,1,0:T(8,128)S(1)} %get-tuple-element.9.info, f32[2,768,768]{2,1,0:T(8,128)S(1)} %get-tuple-element.10.refs_0_, f32[2,256,256]{2,1,0:T(8,128)S(1)} %copy-done.2, f32[2,4,256,256]{3,2,1,0:T(8,128)S(1)} %bitcast.13, ...), custom_call_target="tpu_custom_call" | custom-call | bytes 30000000 | tf_op jit(solution)/shard_map/project/pallas_call | solution.py:473
  51.1 0.0 copy-done.1
  51.1 53.9 %update.1.ext = f32[2,768,768]{2,1,0:T(8,128)S(1)} custom-call(f32[2,768,768]{2,1,0:T(8,128)S(1)} %get-tuple-element.11.refs_0_, f32[2,512,512]{2,1,0:T(8,128)S(1)} %copy-done.1, f32[512,512]{1,0:T(8,128)S(1)} %get-tuple-element.12.refs_2_), custom_call_target="tpu_custom_call" | custom-call | bytes 150000000 | tf_op jit(solution)/shard_map/update/pallas_call | solution.py:489
  105.0 4.5 %renew.1 = (f32[2,4,256,256]{3,2,1,0:T(8,128)}, f32[2,512,512]{2,1,0:T(8,128)}) custom-call(s32[3,3,8,128]{3,2,1,0:T(8,128)S(1)} %get-tuple-element.9.info, f32[2,768,768]{2,1,0:T(8,128)S(1)} %update.1.ext, f32[2,256,256]{2,1,0:T(8,128)S(1)} %copy-done.2, f32[2,4,256,256]{3,2,1,0:T(8,128)S(1)} %get-tuple-element.13.base), custom_call_target="tpu_custom_call" | custom-call | tf_op jit(solution)/shard_map/renew/pallas_call | solution.py:500
  (1 shorter events, 0.0 us)
Async XLA Ops:
  2.0 1.6 %copy-start = (f32[2,512,512]{2,1,0:T(8,128)S(1)}, f32[2,512,512]{2,1,0:T(8,128)}, u32[]{:S(2)}) copy-start(f32[2,512,512]{2,1,0:T(8,128)} %refs_1_.3) | copy-start | bytes 6291460
  3.6 27.1 %copy-start.2 = (f32[2,256,256]{2,1,0:T(8,128)S(1)}, f32[2,256,256]{2,1,0:T(8,128)}, u32[]{:S(2)}) copy-start(f32[2,256,256]{2,1,0:T(8,128)} %probe.1) | copy-start | bytes 1572868
  3.6 27.1 %copy-start.4 = (f32[1,1,4,256,256]{4,3,2,1,0:T(8,128)S(1)}, f32[1,1,4,256,256]{4,3,2,1,0:T(8,128)}, u32[]{:S(2)}) copy-start(f32[1,1,4,256,256]{4,3,2,1,0:T(8,128)} %param.13) | copy-start | bytes 3145732
  3.6 27.1 %copy-start.5 = (bf16[4,256,256]{2,1,0:T(8,128)(2,1)S(1)}, bf16[4,256,256]{2,1,0:T(8,128)(2,1)}, u32[]{:S(2)}) copy-start(bf16[4,256,256]{2,1,0:T(8,128)(2,1)} %constant.10.clone.refs_4_) | copy-start | bytes 1572868
  30.7 1.6 %copy-start.3 = (f32[2,1,1,4,256,256]{5,4,3,2,1,0:T(8,128)S(1)}, f32[2,1,1,4,256,256]{5,4,3,2,1,0:T(8,128)}, u32[]{:S(2)}) copy-start(f32[2,1,1,4,256,256]{5,4,3,2,1,0:T(8,128)} %param.12) | copy-start | bytes 6291460
  32.3 0.9 copy-start.6
  33.3 0.9 copy-start.7
  34.2 0.9 copy-start.8
  35.1 15.9 %copy-start.1 = (f32[2,512,512]{2,1,0:T(8,128)S(1)}, f32[2,512,512]{2,1,0:T(8,128)}, u32[]{:S(2)}) copy-start(f32[2,512,512]{2,1,0:T(8,128)} %refs_1_.3) | copy-start | bytes 6291460
where the time goes:
time: 109 us; the launch traced here: 110 us
  Pallas kernels  101 us (93%)
  local copies, waits for them, and re-layouts  6.68 us (6%)
  between operations  1.35 us (1%)
    pallas_call x1, Pallas kernels, shards(): pl.pallas_call(functools.partial(update_kernel, tile, half), out_shape=sd...  53.9 us
    pallas_call x1, Pallas kernels, shards(): pl.pallas_call(functools.partial(halo_kernel, tile, half), out_shape=(sd(...  27.1 us
    pallas_call x1, Pallas kernels, shards(): pl.pallas_call(functools.partial(project_kernel, tile, half), out_shape=(...  15.9 us
    unnamed x18, local copies, waits for them, and re-layouts  6 us
    pallas_call x1, Pallas kernels, shards(): pl.pallas_call(functools.partial(dual_kernel, tile, half), out_shape=(sd(...  4.5 us

commit v1 on v0

--- a/solution.py
+++ b/solution.py
@@ -38,8 +38,9 @@
     tw = 2.0 * math.pi * k / size
     ct, st = np.cos(tw).astype(np.float32), np.sin(tw).astype(np.float32)
     rows = np.stack([np.broadcast_to(ct[:, None], (n, size)), np.broadcast_to(st[:, None], (n, size))])
-    cols = np.stack([np.broadcast_to(ct[None, :], (size, n)), np.broadcast_to(st[None, :], (size, n))])
-    return [jnp.asarray(np.stack(parts)), jnp.asarray(perm.astype(BF16)), jnp.asarray(rows), jnp.asarray(cols)]
+    both = np.broadcast_to(np.concatenate([ct, st])[None, :], (n, size))
+    waves = np.concatenate([rows, both[None]]).astype(np.float32)
+    return [jnp.asarray(np.stack(parts + [perm.astype(BF16)])), jnp.asarray(waves)]
 
 
 def split(x):
@@ -328,8 +329,8 @@
 
 
 def project_kernel(tile, half, info, *refs):
-    ext, probe, dual, amp, wt, perm, twr, twc = refs[:8]
-    base, acc, weight, heavy, power, strips = refs[8:]
+    dual, ext, probe, amp, wt, tw = refs[:6]
+    base, acc, weight, heavy, power, strips = refs[6:]
     slots = dual.shape[1]
     size = 2 * half
     acc[...] = jnp.zeros_like(acc)
@@ -343,73 +344,91 @@
         base[:, slot] = dual[:, slot]
         return carry
 
-    def step(slot, carry):
-        top = info[1, 1, 0, slot]
-        left = info[1, 1, 0, slots + slot]
-        pr, pi = probe[0], probe[1]
-        sr = load_window(ext, 0, top, left, size)
-        si = load_window(ext, 1, top, left, size)
-        re = pr * sr - pi * si + dual[0, slot]
-        im = pr * si + pi * sr + dual[1, slot]
+    def many(slots_at):
+        tops = [info[1, 1, 0, at] for at in slots_at]
+        lefts = [info[1, 1, 0, slots + at] for at in slots_at]
         fh, fl, ih, il = wt[0], wt[1], wt[2], wt[3]
-        cr, sr_ = twr[0], twr[1]
-        cc, sc = twc[0], twc[1]
-        dr, di = re[:half] - re[half:], im[:half] - im[half:]
-        x = cat(
-            [
-                cat([re[:half] + re[half:], dr * cr + di * sr_], 1),
-                cat([im[:half] + im[half:], di * cr - dr * sr_], 1),
-            ],
-            0,
-        )
-        y = left_dot(fh, fl, x)
-        re = cat([y[:half, :size], y[:half, size:]], 0)
-        im = cat([y[half:, :size], y[half:, size:]], 0)
-        dr, di = re[:, :half] - re[:, half:], im[:, :half] - im[:, half:]
-        x = cat(
-            [
-                cat([re[:, :half] + re[:, half:], im[:, :half] + im[:, half:]], 1),
-                cat([dr * cc + di * sc, di * cc - dr * sc], 1),
-            ],
-            0,
-        )
-        s = right_dot(x, ih, il)
-        for c in range(size // LANES):
-            strips[c] = amp[slot, :, c * LANES : (c + 1) * LANES]
-        a = cat(
-            [
-                cat([strips[c, pl.ds(first, half, stride=2), :] for c in range(size // LANES)], 1)
-                for first in range(2)
-            ],
-            0,
-        )
-        ah, al = split(a)
-        a = dot(ah, perm[...]) + dot(al, perm[...])
-        a = cat([a[:, :half], a[:, half:]], 0)
-        sre, sim = s[:, :half], s[:, half:]
-        fac = a * lax.rsqrt(jnp.maximum(sre * sre + sim * sim, FLOOR * FLOOR))
-        x = cat([sre * fac, sim * fac], 1)
-        z = right_dot(x, fh, fl)
-        er, ei = z[:size, :half], z[:size, half:]
-        orr, oi = z[size:, :half], z[size:, half:]
-        tr, ti = orr * cc - oi * sc, oi * cc + orr * sc
-        re = cat([er + tr, er - tr], 1)
-        im = cat([ei + ti, ei - ti], 1)
-        x = cat([cat([re[:half], re[half:]], 1), cat([im[:half], im[half:]], 1)], 0)
-        y = left_dot(ih, il, x)
-        er, ei = y[:half, :size], y[half:, :size]
-        orr, oi = y[:half, size:], y[half:, size:]
-        tr, ti = orr * cr - oi * sr_, oi * cr + orr * sr_
-        dr = cat([er + tr, er - tr], 0) - dual[0, slot]
-        di = cat([ei + ti, ei - ti], 0) - dual[1, slot]
-        base[0, slot] = -dr
-        base[1, slot] = -di
-        add_window(acc, 0, top, left, pr * dr + pi * di)
-        add_window(acc, 1, top, left, pr * di - pi * dr)
+        cr, sr = tw[0], tw[1]
+        cc = jnp.broadcast_to(tw[2, :1, :half], (size, half))
+        sc = jnp.broadcast_to(tw[2, :1, half:], (size, half))
+        n = range(len(slots_at))
+        x = []
+        for at, top, left in zip(slots_at, tops, lefts):
+            pr, pi = probe[0], probe[1]
+            wr = load_window(ext, 0, top, left, size)
+            wi = load_window(ext, 1, top, left, size)
+            re = pr * wr - pi * wi + dual[0, at]
+            im = pr * wi + pi * wr + dual[1, at]
+            dr, di = re[:half] - re[half:], im[:half] - im[half:]
+            x.append(
+                cat(
+                    [
+                        cat([re[:half] + re[half:], dr * cr + di * sr], 1),
+                        cat([im[:half] + im[half:], di * cr - dr * sr], 1),
+                    ],
+                    0,
+                )
+            )
+        y = left_dot(fh, fl, cat(x, 1))
+        y = [y[:, 2 * size * i : 2 * size * (i + 1)] for i in n]
+        x = []
+        for v in y:
+            re = cat([v[:half, :size], v[:half, size:]], 0)
+            im = cat([v[half:, :size], v[half:, size:]], 0)
+            dr, di = re[:, :half] - re[:, half:], im[:, :half] - im[:, half:]
+            x.append(cat([re[:, :half] + re[:, half:], im[:, :half] + im[:, half:]], 1))
+            x.append(cat([dr * cc + di * sc, di * cc - dr * sc], 1))
+        s = right_dot(cat(x, 0), ih, il)
+        s = [s[2 * size * i : 2 * size * (i + 1)] for i in n]
+        rows = []
+        for i, at in enumerate(slots_at):
+            for c in range(size // LANES):
+                strips[i, c] = amp[at, :, c * LANES : (c + 1) * LANES]
+            for first in range(2):
+                rows.append(cat([strips[i, c, pl.ds(first, half, stride=2), :] for c in range(size // LANES)], 1))
+        ah, al = split(cat(rows, 0))
+        a = dot(ah, wt[4]) + dot(al, wt[4])
+        x = []
+        for i in n:
+            b = a[size * i : size * (i + 1)]
+            b = cat([b[:, :half], b[:, half:]], 0)
+            re, im = s[i][:, :half], s[i][:, half:]
+            fac = b * lax.rsqrt(jnp.maximum(re * re + im * im, FLOOR * FLOOR))
+            x.append(cat([re * fac, im * fac], 1))
+        z = right_dot(cat(x, 0), fh, fl)
+        x = []
+        for i in n:
+            v = z[2 * size * i : 2 * size * (i + 1)]
+            er, ei = v[:size, :half], v[:size, half:]
+            our, oui = v[size:, :half], v[size:, half:]
+            tr, ti = our * cc - oui * sc, oui * cc + our * sc
+            re = cat([er + tr, er - tr], 1)
+            im = cat([ei + ti, ei - ti], 1)
+            x.append(cat([cat([re[:half], re[half:]], 1), cat([im[:half], im[half:]], 1)], 0))
+        y = left_dot(ih, il, cat(x, 1))
+        for i, (at, top, left) in enumerate(zip(slots_at, tops, lefts)):
+            v = y[:, 2 * size * i : 2 * size * (i + 1)]
+            er, ei = v[:half, :size], v[half:, :size]
+            our, oui = v[:half, size:], v[half:, size:]
+            tr, ti = our * cr - oui * sr, oui * cr + our * sr
+            dr = cat([er + tr, er - tr], 0) - dual[0, at]
+            di = cat([ei + ti, ei - ti], 0) - dual[1, at]
+            base[0, at] = -dr
+            base[1, at] = -di
+            pr, pi = probe[0], probe[1]
+            add_window(acc, 0, top, left, pr * dr + pi * di)
+            add_window(acc, 1, top, left, pr * di - pi * dr)
+
+    def pair(index, carry):
+        many([2 * index, 2 * index + 1])
         return carry
 
     lax.fori_loop(live, slots, skip, 0)
-    lax.fori_loop(0, live, step, 0)
+    lax.fori_loop(0, live // 2, pair, 0)
+
+    @pl.when(live % 2 == 1)
+    def _():
+        many([live - 1])
 
 
 def dual_kernel(tile, half, info, ext, probe, base, out, new, ready, sems):
@@ -473,17 +492,17 @@
     base, acc, weight = pl.pallas_call(
         functools.partial(project_kernel, tile, half),
         out_shape=(sd(2, slots, size, size), sd(2, wide, wide), sd(tile, tile)),
-        in_specs=[SM] + [VM] * 8,
+        in_specs=[SM] + [VM] * 6,
         out_specs=(VM, VM, VM),
         scratch_shapes=[
             pltpu.VMEM((1, tile + 2 * size, tile + 2 * size), F32),
             pltpu.VMEM((size, size), F32),
-            pltpu.VMEM((size // LANES, size, LANES), F32),
+            pltpu.VMEM((2, size // LANES, size, LANES), F32),
         ],
-        compiler_params=pltpu.CompilerParams(vmem_limit_bytes=16 * MIB),
+        compiler_params=pltpu.CompilerParams(vmem_limit_bytes=20 * MIB),
         cost_estimate=cost(30_000_000),
         name="project",
-    )(infos, frame, probe, lam, amps, *tables(size))
+    )(infos, lam, frame, probe, amps, *tables(size))
 
     strip, side, end = (2, half, wide), (2, mid, half), (2, 2, half, half)
     frame = pl.pallas_call(

time: 109 us -> 105 us (0.963); the launches traced: 110 us -> 103 us
  Pallas kernels: 101 us -> 96.5 us
  local copies, waits for them, and re-layouts: 6.68 us -> 4.96 us
    pallas_call x1, Pallas kernels: 15.9 us -> 6.89 us  [shards(): pl.pallas_call(functools.partial(project_kernel, tile, half), out_shape=(...]
    pallas_call x1, Pallas kernels: 53.9 us -> 59.4 us  [shards(): pl.pallas_call(functools.partial(update_kernel, tile, half), out_shape=sd...]
    unnamed x18 -> x14, local copies, waits for them, and re-layouts: 6 us -> 4.28 us
    pallas_call x1, Pallas kernels: 4.5 us -> 3.19 us  [shards(): pl.pallas_call(functools.partial(dual_kernel, tile, half), out_shape=(sd(...]
where the time goes in v1:
time: 105 us; the launch traced here: 103 us
  Pallas kernels  96.5 us (92%)
  local copies, waits for them, and re-layouts  4.96 us (5%)
  between operations  1.35 us (1%)
    pallas_call x1, Pallas kernels, shards(): pl.pallas_call(functools.partial(update_kernel, tile, half), out_shape=sd...  59.4 us
    pallas_call x1, Pallas kernels, shards(): pl.pallas_call(functools.partial(halo_kernel, tile, half), out_shape=(sd(...  27.1 us
    pallas_call x1, Pallas kernels, shards(): pl.pallas_call(functools.partial(project_kernel, tile, half), out_shape=(...  6.89 us
    unnamed x14, local copies, waits for them, and re-layouts  4.28 us
    pallas_call x1, Pallas kernels, shards(): pl.pallas_call(functools.partial(dual_kernel, tile, half), out_shape=(sd(...  3.19 us

profile of v1, /device:TPU:13, one launch (start us, length us, event | category | flops | bytes accessed | tf_op | source)
XLA Modules:
  0.0 102.9 jit_solution(14307723506285772667)
XLA Ops:
  1.3 0.7 slice_bitcast_fusion.1
  2.0 0.1 add_bitcast_fusion
  2.0 0.0 copy-start
  2.0 1.6 %copy-done = f32[2,512,512]{2,1,0:T(8,128)S(1)} copy-done((f32[2,512,512]{2,1,0:T(8,128)S(1)}, f32[2,512,512]{2,1,0:T(8,128)}, u32[]{:S(2)}) %copy-start) | copy-done | bytes 2097176
  3.6 0.0 copy-start.2
  3.6 0.0 copy-start.4
  3.6 0.0 copy-start.6
  3.6 27.1 %halo.1 = (f32[2,768,768]{2,1,0:T(8,128)S(1)}, s32[3,3,8,128]{3,2,1,0:T(8,128)S(1)}) custom-call(f32[2,512,512]{2,1,0:T(8,128)S(1)} %copy-done, s32[4,8,128]{2,1,0:T(8,128)S(1)} %pad.4.info), custom_call_target="tpu_custom_call" | custom-call | bytes 80000000 | tf_op jit(solution)/shard_map/halo/pallas_call | solution.py:480
  30.7 0.0 copy-done.2
  30.7 0.0 copy-done.4
  30.7 0.0 copy-done.6
  30.7 0.0 copy-start.3
  30.8 1.6 %copy-done.3 = f32[2,1,1,4,256,256]{5,4,3,2,1,0:T(8,128)S(1)} copy-done((f32[2,1,1,4,256,256]{5,4,3,2,1,0:T(8,128)S(1)}, f32[2,1,1,4,256,256]{5,4,3,2,1,0:T(8,128)}, u32[]{:S(2)}) %copy-start.3) | copy-done | bytes 2097176
  32.3 0.0 copy-start.5
  32.3 1.1 %copy-done.5 = bf16[5,256,256]{2,1,0:T(8,128)(2,1)S(1)} copy-done((bf16[5,256,256]{2,1,0:T(8,128)(2,1)S(1)}, bf16[5,256,256]{2,1,0:T(8,128)(2,1)}, u32[]{:S(2)}) %copy-start.5) | copy-done | bytes 655384
  33.4 0.0 copy-start.1
  33.4 6.9 %project.1 = (f32[2,4,256,256]{3,2,1,0:T(8,128)S(1)}, f32[2,768,768]{2,1,0:T(8,128)S(1)}, f32[512,512]{1,0:T(8,128)S(1)}) custom-call(s32[3,3,8,128]{3,2,1,0:T(8,128)S(1)} %get-tuple-element.9.info, f32[2,4,256,256]{3,2,1,0:T(8,128)S(1)} %bitcast.13, f32[2,768,768]{2,1,0:T(8,128)S(1)} %get-tuple-element.10.refs_1_, f32[2,256,256]{2,1,0:T(8,128)S(1)} %copy-done.2, ...), custom_call_target="tpu_custom_call" | custom-call | bytes 30000000 | tf_op jit(solution)/shard_map/project/pallas_call | solution.py:492
  40.3 0.0 copy-done.1
  40.3 59.4 %update.1.ext = f32[2,768,768]{2,1,0:T(8,128)S(1)} custom-call(f32[2,768,768]{2,1,0:T(8,128)S(1)} %get-tuple-element.11.refs_0_, f32[2,512,512]{2,1,0:T(8,128)S(1)} %copy-done.1, f32[512,512]{1,0:T(8,128)S(1)} %get-tuple-element.12.refs_2_), custom_call_target="tpu_custom_call" | custom-call | bytes 150000000 | tf_op jit(solution)/shard_map/update/pallas_call | solution.py:508
  99.7 3.2 %renew.1 = (f32[2,4,256,256]{3,2,1,0:T(8,128)}, f32[2,512,512]{2,1,0:T(8,128)}) custom-call(s32[3,3,8,128]{3,2,1,0:T(8,128)S(1)} %get-tuple-element.9.info, f32[2,768,768]{2,1,0:T(8,128)S(1)} %update.1.ext, f32[2,256,256]{2,1,0:T(8,128)S(1)} %copy-done.2, f32[2,4,256,256]{3,2,1,0:T(8,128)S(1)} %get-tuple-element.13.base), custom_call_target="tpu_custom_call" | custom-call | tf_op jit(solution)/shard_map/renew/pallas_call | solution.py:519
  (1 shorter events, 0.0 us)
Async XLA Ops:
  2.0 1.6 %copy-start = (f32[2,512,512]{2,1,0:T(8,128)S(1)}, f32[2,512,512]{2,1,0:T(8,128)}, u32[]{:S(2)}) copy-start(f32[2,512,512]{2,1,0:T(8,128)} %refs_1_.1) | copy-start | bytes 6291460
  3.6 27.1 %copy-start.2 = (f32[2,256,256]{2,1,0:T(8,128)S(1)}, f32[2,256,256]{2,1,0:T(8,128)}, u32[]{:S(2)}) copy-start(f32[2,256,256]{2,1,0:T(8,128)} %probe.1) | copy-start | bytes 1572868
  3.6 27.1 %copy-start.4 = (f32[1,1,4,256,256]{4,3,2,1,0:T(8,128)S(1)}, f32[1,1,4,256,256]{4,3,2,1,0:T(8,128)}, u32[]{:S(2)}) copy-start(f32[1,1,4,256,256]{4,3,2,1,0:T(8,128)} %param.11) | copy-start | bytes 3145732
  3.6 27.1 %copy-start.6 = (f32[3,128,256]{2,1,0:T(8,128)S(1)}, f32[3,128,256]{2,1,0:T(8,128)}, u32[]{:S(2)}) copy-start(f32[3,128,256]{2,1,0:T(8,128)} %constant.7.clone.refs_5_) | copy-start | bytes 1179652
  30.7 1.6 %copy-start.3 = (f32[2,1,1,4,256,256]{5,4,3,2,1,0:T(8,128)S(1)}, f32[2,1,1,4,256,256]{5,4,3,2,1,0:T(8,128)}, u32[]{:S(2)}) copy-start(f32[2,1,1,4,256,256]{5,4,3,2,1,0:T(8,128)} %param.10) | copy-start | bytes 6291460
  32.3 1.1 %copy-start.5 = (bf16[5,256,256]{2,1,0:T(8,128)(2,1)S(1)}, bf16[5,256,256]{2,1,0:T(8,128)(2,1)}, u32[]{:S(2)}) copy-start(bf16[5,256,256]{2,1,0:T(8,128)(2,1)} %constant.6.clone.refs_4_) | copy-start | bytes 1966084
  33.4 6.9 %copy-start.1 = (f32[2,512,512]{2,1,0:T(8,128)S(1)}, f32[2,512,512]{2,1,0:T(8,128)}, u32[]{:S(2)}) copy-start(f32[2,512,512]{2,1,0:T(8,128)} %refs_1_.1) | copy-start | bytes 6291460
